TPU v7x, 32 devices: a whole 2x2x4 slice. The times are simulated.
32 devices in a mesh: dp: 16 (over z, y, core), seq: 2 (over x).
Axes of the slice: x: 2, y: 2, z: 4, core: 2. Of those that a mesh axis runs over, the one named last changes fastest.
Arguments:
- queries: bfloat16 [4096, 1536], P(('dp', 'seq')), may hold values from -5 to 5
- keys: bfloat16 [4096, 1536], P(('dp', 'seq')), may hold values from -5 to 5
- values: bfloat16 [4096, 1536], P(('dp', 'seq')), may hold values from -6 to 6
- upstream: bfloat16 [4096, 1536], P(('dp', 'seq')), may hold values from -6 to 6
- out_weight: bfloat16 [1536, 1536], P('dp'), may hold values from -0.15625 to 0.15625
- clip_shape: int32 [16, 2, 3], P('dp'), may hold values from 1 to 3, as said below
- slot_tile: int32 [16, 8], P('dp'), may hold values from 0 to 7, each once within a row
Outputs:
- mixed_out: bfloat16 [4096, 1536], P(('dp', 'seq'))
- query_grad: bfloat16 [4096, 1536], P(('dp', 'seq'))
- key_grad: bfloat16 [4096, 1536], P(('dp', 'seq'))
- value_grad: bfloat16 [4096, 1536], P(('dp', 'seq'))
- weight_grad: float32 [1536, 1536], P('dp')
Inputs may be any that keep to these rules, and one draw needn't show every extreme that they name: `clip_shape`: in every batch the clips' tile counts add up to 8; a clip is 1 or 2 tiles long in time and 2 tiles high.
All inputs are finite; a program needn't handle non-finite values.
Results may differ from a plain program's by a relative error of at most 0.02.
Values may be sent and summed in bfloat16 or wider, within the bound.
No kernel may reach another device: no remote copies, remote signals or barrier semaphores. Data moves between devices by JAX's collectives and lax.ppermute only.
A program may use at most 128 MiB of HBM per device.

v0:
```python
import jax
import jax.numpy as jnp
from jax import lax
from jax.sharding import PartitionSpec as P

HEADS = 12
HEAD_DIM = 128
TILE = 32


def tile_place(clip_dims, tile_ids):
    clip_sizes = clip_dims[:, 0] * clip_dims[:, 1] * clip_dims[:, 2]
    clip_starts = jnp.cumsum(clip_sizes) - clip_sizes
    clip_of = jnp.sum((tile_ids[:, None] >= clip_starts[None, :]).astype(jnp.int32), axis=1) - 1
    chooser = (clip_of[:, None] == jnp.arange(clip_dims.shape[0], dtype=jnp.int32)[None, :]).astype(
        jnp.int32
    )
    first_tile = jnp.sum(chooser * clip_starts[None, :], axis=1)
    high_tiles = jnp.sum(chooser * clip_dims[None, :, 1], axis=1)
    wide_tiles = jnp.sum(chooser * clip_dims[None, :, 2], axis=1)
    offset = tile_ids - first_tile
    return (
        clip_of,
        offset // (wide_tiles * high_tiles),
        offset // wide_tiles % high_tiles,
        offset % wide_tiles,
    )


def tile_window(place_rows, place_cols):
    inside = place_rows[0][:, None] == place_cols[0][None, :]
    for dimension in range(1, 4):
        inside = inside & (
            jnp.abs(place_rows[dimension][:, None] - place_cols[dimension][None, :]) <= 1
        )
    return inside


def per_device(queries, keys, values, upstream, out_weight, clip_shape, slot_tile):
    row_count = queries.shape[0]
    feat_count = queries.shape[1]
    scaling = HEAD_DIM ** (-0.5)
    clip_dims = clip_shape[0]
    slot_list = slot_tile[0]
    local_tiles = row_count // TILE
    own_seat = lax.axis_index("seq")
    own_slots = lax.dynamic_slice_in_dim(slot_list, own_seat * local_tiles, local_tiles)
    own_tokens = own_slots[jnp.arange(row_count, dtype=jnp.int32) // TILE]
    all_tokens = slot_list[jnp.arange(slot_list.shape[0] * TILE, dtype=jnp.int32) // TILE]
    own_place = tile_place(clip_dims, own_tokens)
    all_place = tile_place(clip_dims, all_tokens)
    allowed = tile_window(own_place, all_place)
    full_weight = lax.all_gather(out_weight, "dp", axis=0, tiled=True)
    key_all, value_all = (
        lax.all_gather(keys, "seq", axis=0, tiled=True),
        lax.all_gather(values, "seq", axis=0, tiled=True),
    )
    group_tokens = key_all.shape[0]
    query3 = queries.reshape(row_count, HEADS, HEAD_DIM)
    key_all3 = key_all.reshape(group_tokens, HEADS, HEAD_DIM)
    value_all3 = value_all.reshape(group_tokens, HEADS, HEAD_DIM)
    scores = (
        jnp.einsum("ihd,jhd->hij", query3, key_all3, preferred_element_type=jnp.float32) * scaling
    )
    scores = jnp.where(allowed[None], scores, -jnp.inf)
    row_max = jnp.max(scores, axis=2)
    exponent = jnp.exp(scores - row_max[:, :, None])
    row_sum = jnp.sum(exponent, axis=2)
    weights = exponent.astype(jnp.bfloat16)
    mixed = (
        jnp.einsum("hij,jhd->ihd", weights, value_all3, preferred_element_type=jnp.float32)
        / jnp.transpose(row_sum)[:, :, None]
    )
    attended = mixed.reshape(row_count, feat_count).astype(jnp.bfloat16)
    mixed_out = jnp.einsum(
        "id,od->io", attended, full_weight, preferred_element_type=jnp.float32
    ).astype(jnp.bfloat16)
    grad_out = jnp.dot(upstream, full_weight, preferred_element_type=jnp.float32).astype(
        jnp.bfloat16
    )
    grad3 = grad_out.reshape(row_count, HEADS, HEAD_DIM)
    attended3 = attended.reshape(row_count, HEADS, HEAD_DIM)
    inner_sum = jnp.transpose(
        jnp.sum(grad3.astype(jnp.float32) * attended3.astype(jnp.float32), axis=2)
    )
    log_total = row_max + jnp.log(row_sum)
    prob_full = jnp.exp(scores - log_total[:, :, None])
    slope = jnp.einsum("ihd,jhd->hij", grad3, value_all3, preferred_element_type=jnp.float32)
    score_grad = (prob_full * (slope - inner_sum[:, :, None])).astype(jnp.bfloat16)
    query_grad = (
        (
            jnp.einsum("hij,jhd->ihd", score_grad, key_all3, preferred_element_type=jnp.float32)
            * scaling
        )
        .reshape(row_count, feat_count)
        .astype(jnp.bfloat16)
    )
    prob_low = prob_full.astype(jnp.bfloat16)
    key_part = (
        jnp.einsum("hij,ihd->jhd", score_grad, query3, preferred_element_type=jnp.float32) * scaling
    )
    value_part = jnp.einsum("hij,ihd->jhd", prob_low, grad3, preferred_element_type=jnp.float32)
    key_value_grad = lax.psum_scatter(
        jnp.concatenate(
            [
                key_part.reshape(row_count * lax.axis_size("seq"), feat_count),
                value_part.reshape(row_count * lax.axis_size("seq"), feat_count),
            ],
            axis=1,
        ),
        "seq",
        scatter_dimension=0,
        tiled=True,
    )
    key_grad = key_value_grad[:, :feat_count].astype(jnp.bfloat16)
    value_grad = key_value_grad[:, feat_count:].astype(jnp.bfloat16)
    grad_piece = lax.psum_scatter(
        jnp.einsum("io,id->od", upstream, attended, preferred_element_type=jnp.float32),
        "dp",
        scatter_dimension=0,
        tiled=True,
    )
    weight_grad = lax.psum(grad_piece, "seq")
    return (mixed_out, query_grad, key_grad, value_grad, weight_grad)


def solution(mesh):
    return jax.shard_map(
        per_device,
        mesh=mesh,
        in_specs=(
            P(("dp", "seq"), None),
            P(("dp", "seq"), None),
            P(("dp", "seq"), None),
            P(("dp", "seq"), None),
            P("dp", None),
            P("dp", None, None),
            P("dp", None),
        ),
        out_specs=(
            P(("dp", "seq"), None),
            P(("dp", "seq"), None),
            P(("dp", "seq"), None),
            P(("dp", "seq"), None),
            P("dp", None),
        ),
        check_vma=False,
    )
```

profile of v0, /device:TPU:0, one launch (start us, length us, event | category | flops | bytes accessed | tf_op | source)
XLA Modules:
  0.0 287.7 jit_solution(4399860673712116079)
XLA Ops:
  7.2 0.0 copy-start
  7.2 0.0 copy-start.7
  7.2 0.0 all-gather.2.cloned.1.call-start
  7.2 0.7 all-gather.2.cloned.1.call-update
  7.9 0.0 reduce-scatter.7.cloned.1.call-start
  8.0 1.0 slice_reduce_fusion.1
  9.0 0.1 reduce
  9.1 1.2 copy.47
  10.4 0.0 copy-start.3
  10.4 1.4 copy.48
  11.7 0.0 copy-done.7
  11.8 0.0 copy-start.10
  11.8 12.8 %all_gather.10 = bf16[256,1536]{1,0:T(8,128)(2,1)S(1)} all-gather(bf16[128,1536]{1,0:T(8,128)(2,1)S(1)} %copy-done.7), channel_id=1, replica_groups=mesh['dp'=16,'seq'=2] {'seq'}, dimensions={0}, use_global_device_ids=true | all-gather | bytes 1179648 | tf_op jit(solution)/shard_map/all_gather | solution.py:56
  24.5 1.2 copy.51
  25.7 0.0 copy-done.10
  25.7 0.1 constant_dynamic-slice_fusion
  25.8 0.7 fusion.18
  26.5 2.5 fusion.16
  29.0 0.6 fusion.19
  29.6 4.4 %compare_select_fusion.1 = s32[256,1]{0,1:T(1,128)S(1)} fusion(s32[]{:T(128)} %bitcast.7, s32[]{:T(128)} %bitcast.8, s32[]{:T(128)} %bitcast.9, s32[]{:T(128)} %bitcast.10, s32[]{:T(128)} %bitcast.11, s32[]{:T(128)} %bitcast.13, s32[]{:T(128)} %bitcast.12), kind=kLoop, calls=%fused_computation.30 | loop fusion | flops 5888 | bytes 1052 | tf_op jit(solution)/shard_map/gather | solution.py:49
  34.1 0.1 fusion.15
  34.2 0.6 broadcast_select_fusion
  34.8 0.1 fusion.14
  34.9 0.1 select_reduce_fusion.3
  35.0 0.1 select_reduce_fusion
  35.1 11.0 %all_gather.9 = bf16[256,1536]{0,1:T(8,128)(2,1)S(1)} all-gather(bf16[128,1536]{0,1:T(8,128)(2,1)S(1)} %copy.48), channel_id=1, replica_groups=mesh['dp'=16,'seq'=2] {'seq'}, dimensions={0}, use_global_device_ids=true | all-gather | bytes 1179648 | tf_op jit(solution)/shard_map/all_gather | solution.py:55
  46.1 2.8 and_select_fusion.8
  48.8 0.3 and_select_fusion.7
  49.1 0.2 fusion.13
  49.3 0.5 fusion.20
  49.8 0.5 fusion
  50.3 0.0 copy-start.8
  50.3 15.7 %all-gather.2.cloned.1.call-done = bf16[1536,1536]{1,0:T(8,128)(2,1)} async-done(((bf16[96,1536]{1,0:T(8,128)(2,1)}), bf16[1536,1536]{1,0:T(8,128)(2,1)}) %all-gather.2.cloned.1.call-update) | async-done | bytes 4718608 | tf_op jit(solution)/shard_map/all_gather | solution.py:53
  66.0 3.1 %convolution_convert_fusion = bf16[128,1536]{1,0:T(8,128)(2,1)S(1)} fusion(bf16[128,1536]{1,0:T(8,128)(2,1)S(1)} %copy-done, bf16[1536,1536]{1,0:T(8,128)(2,1)} %all-gather.2.cloned.1.call-done), kind=kOutput, calls=%fused_computation.2 | convolution fusion | flops 604176384 | bytes 5505024 | tf_op jit(solution)/shard_map/dot_general | solution.py:78
  69.1 0.2 copy.52
  69.3 0.0 copy-start.2
  69.3 2.4 multiply_reduce_fusion
  71.7 0.7 copy-done.5
  72.5 5.0 %convolution_bitcast_fusion = f32[1536,1536]{0,1:T(8,128)} fusion(bf16[128,1536]{0,1:T(8,128)(2,1)S(1)} %bitcast.70, bf16[128,1536]{1,0:T(8,128)(2,1)S(1)} %copy-done), kind=kOutput, calls=%fused_computation | convolution fusion | flops 603979776 | bytes 10223616 | tf_op jit(solution)/shard_map/io,id->od/dot_general | solution.py:118
  77.5 9.6 %copy.63 = f32[1536,1536]{1,0:T(8,128)} copy(f32[1536,1536]{0,1:T(8,128)} %convolution_bitcast_fusion) | data formatting | bytes 18874368
  87.1 0.0 reduce-scatter.7.cloned.1.call-update
  87.2 0.0 reduce-scatter.5.cloned.1.call-start
  87.2 0.6 copy-done.9
  87.9 0.0 copy-done.2
  87.9 1.6 fusion.6
  89.5 3.1 %copy.56 = f32[256,1536]{1,0:T(8,128)} copy(f32[256,1536]{0,1:T(8,128)} %bitcast.61) | data formatting | bytes 3145728 | tf_op jit(solution)/shard_map/reshape | solution.py:107
  92.5 2.1 multiply_convert_fusion
  94.7 1.5 convolution_multiply_fusion
  96.2 3.4 %copy.55 = f32[256,1536]{1,0:T(8,128)} copy(f32[256,1536]{0,1:T(8,128)} %bitcast.62) | data formatting | bytes 3145728 | tf_op jit(solution)/shard_map/reshape | solution.py:106
  99.5 3.5 %pad_maximum_fusion = f32[256,3072]{1,0:T(8,128)} fusion(f32[256,1536]{1,0:T(8,128)S(1)} %copy-done.1, f32[256,1536]{1,0:T(8,128)} %copy.55), kind=kLoop, calls=%fused_computation.1 | loop fusion | flops 786432 | bytes 6291456 | tf_op jit(solution)/shard_map/concatenate | solution.py:104
  103.0 0.0 reduce-scatter.5.cloned.1.call-update
  103.0 0.0 all-reduce.2.cloned.1.call-start
  103.1 1.0 copy-done.6
  104.0 5.3 %convolution_convert_fusion.1 = bf16[128,1536]{1,0:T(8,128)(2,1)} fusion(bf16[128,1536]{0,1:T(8,128)(2,1)S(1)} %bitcast.71, bf16[1536,1536]{1,0:T(8,128)(2,1)} %all-gather.2.cloned.1.call-done), kind=kOutput, calls=%fused_computation.3 | convolution fusion | flops 604176384 | bytes 5505024 | tf_op jit(solution)/shard_map/id,od->io/dot_general | solution.py:75
  109.3 87.8 %reduce-scatter.7.cloned.1.call-done = f32[96,1536]{1,0:T(8,128)} async-done(((f32[1536,1536]{1,0:T(8,128)}), f32[96,1536]{1,0:T(8,128)}) %reduce-scatter.7.cloned.1.call-update) | async-done | bytes 589840
  197.1 2.2 copy.64
  199.3 0.0 all-reduce.2.cloned.1.call-update
  199.3 0.4 fusion.4
  199.7 0.9 copy.57
  200.6 41.8 %reduce-scatter.5.cloned.1.call-done = f32[128,3072]{1,0:T(8,128)} async-done(((f32[256,3072]{1,0:T(8,128)}), f32[128,3072]{1,0:T(8,128)}) %reduce-scatter.5.cloned.1.call-update) | async-done | bytes 1572880 | tf_op jit(solution)/shard_map/reduce_scatter | solution.py:103
  242.4 1.5 convert.4
  243.9 0.9 fusion.17
  244.9 34.1 %all-reduce.2.cloned.1.call-done = f32[96,1536]{0,1:T(8,128)} async-done(((f32[96,1536]{0,1:T(8,128)}), f32[96,1536]{0,1:T(8,128)}) %all-reduce.2.cloned.1.call-update) | async-done | bytes 589840 | tf_op jit(solution)/shard_map/psum | solution.py:123
  279.0 2.2 copy.58
  (18 shorter events, 0.1 us)
Async XLA Ops:
  7.2 58.8 %copy-start = (bf16[128,1536]{1,0:T(8,128)(2,1)S(1)}, bf16[128,1536]{1,0:T(8,128)(2,1)}, u32[]{:S(2)}) copy-start(bf16[128,1536]{1,0:T(8,128)(2,1)} %param.10) | copy-start | bytes 1179652
  7.2 4.6 %copy-start.7 = (bf16[128,1536]{1,0:T(8,128)(2,1)S(1)}, bf16[128,1536]{1,0:T(8,128)(2,1)}, u32[]{:S(2)}) copy-start(bf16[128,1536]{1,0:T(8,128)(2,1)} %param.9) | copy-start | bytes 1179652
  7.2 58.8 %all-gather.2.cloned.1.call-start = ((), (), s32[]{:S(2)}) async-start(), calls=%async_computation.2 | async-start | bytes 5013504 | tf_op jit(solution)/shard_map/all_gather | solution.py:53
  7.9 189.2 %reduce-scatter.7.cloned.1.call-start = ((), (), s32[]{:S(2)}) async-start(), calls=%async_computation.5 | async-start | bytes 10027008
  10.4 38.9 %copy-start.3 = (bf16[128,1536]{0,1:T(8,128)(2,1)}, bf16[128,1536]{0,1:T(8,128)(2,1)S(1)}, u32[]{:S(2)}) copy-start(bf16[128,1536]{0,1:T(8,128)(2,1)S(1)} %copy.47) | copy-start | bytes 1179652
  11.8 14.0 %copy-start.10 = (s32[1,8]{1,0:T(1,128)S(1)}, s32[1,8]{1,0:T(1,128)}, u32[]{:S(2)}) copy-start(s32[1,8]{1,0:T(1,128)} %param.13) | copy-start | bytes 100
  50.3 19.0 %copy-start.8 = (f32[12,128]{1,0:T(8,128)}, f32[12,128]{1,0:T(8,128)S(1)}, u32[]{:S(2)}) copy-start(f32[12,128]{1,0:T(8,128)S(1)} %fusion) | copy-start | bytes 18436
  69.3 18.5 %copy-start.2 = (bf16[128,1536]{0,1:T(8,128)(2,1)}, bf16[128,1536]{0,1:T(8,128)(2,1)S(1)}, u32[]{:S(2)}) copy-start(bf16[128,1536]{0,1:T(8,128)(2,1)S(1)} %copy.52) | copy-start | bytes 1179652
  71.7 0.7 copy-start.5
  87.1 0.7 copy-start.9
  87.2 155.3 %reduce-scatter.5.cloned.1.call-start = ((), (), s32[]{:S(2)}) async-start(), calls=%async_computation.3 | async-start | bytes 4718592 | tf_op jit(solution)/shard_map/reduce_scatter | solution.py:103
  89.5 3.1 %copy-start.11 = (f32[128,12]{0,1:T(8,128)S(1)}, f32[128,12]{0,1:T(8,128)}, u32[]{:S(2)}) copy-start(f32[128,12]{0,1:T(8,128)} %get-tuple-element.57) | copy-start | bytes 18436
  92.5 2.1 copy-start.4
  96.2 3.4 %copy-start.1 = (f32[256,1536]{1,0:T(8,128)S(1)}, f32[256,1536]{1,0:T(8,128)}, u32[]{:S(2)}) copy-start(f32[256,1536]{1,0:T(8,128)} %copy.56) | copy-start | bytes 4718596
  103.0 1.0 copy-start.6
  103.0 176.0 %all-reduce.2.cloned.1.call-start = ((), (), s32[]{:S(2)}) async-start(), calls=%async_computation.4 | async-start | bytes 1572864 | tf_op jit(solution)/shard_map/psum | solution.py:123
Sparse Core Ops, SparseCore 0:
  10.3 55.6 all-gather.1
  87.3 109.7 reduce-scatter.6
  199.3 43.0 reduce-scatter.4
  244.6 34.3 all-reduce.1
where the time goes:
time: 289 us; the launch traced here: 288 us
  waiting for transfers between devices  180 us (62%)
  local copies, waits for them, and re-layouts  30.1 us (10%)
  blocking collectives  23.7 us (8%)
  matrix products  21.9 us (8%)
  other arithmetic  17.8 us (6%)
  between operations  14 us (5%)
    unnamed x5, waiting for transfers between devices  88.5 us
    reduce_scatter x1, waiting for transfers between devices, per_device(): lax.psum_scatter(jnp.concatenate([key_part.reshape(row_count * lax.axis_s...  41.8 us
    psum x1, waiting for transfers between devices, per_device(): weight_grad = lax.psum(grad_piece, 'seq')  34.1 us
    unnamed x30, local copies, waits for them, and re-layouts  19.9 us
    all_gather x1, waiting for transfers between devices, per_device(): full_weight = lax.all_gather(out_weight, 'dp', axis=0, tiled=True)  15.7 us
    all_gather x1, blocking collectives, per_device(): lax.all_gather(values, 'seq', axis=0, tiled=True)  12.8 us
    all_gather x1, blocking collectives, per_device(): lax.all_gather(keys, 'seq', axis=0, tiled=True)  11 us
  transfers between devices with their start and end apart: 4, of which 4 were waited for; matrix products, arithmetic and copies ran while one was open for 16% of the time, Pallas kernels for 0%

commit v1 on v0

--- a/solution.py
+++ b/solution.py
@@ -120,7 +120,7 @@
         scatter_dimension=0,
         tiled=True,
     )
-    weight_grad = lax.psum(grad_piece, "seq")
+    weight_grad = jnp.sum(lax.all_gather(grad_piece, "seq"), axis=0)
     return (mixed_out, query_grad, key_grad, value_grad, weight_grad)
 
 

time: 289 us -> 276 us (0.955)
  waiting for transfers between devices: 180 us -> 171 us
  local copies, waits for them, and re-layouts: 30.1 us -> 24.7 us
    reduce_scatter x0 -> x1, waiting for transfers between devices: none -> 94 us  [per_device(): lax.psum_scatter(jnp.einsum('io,id->od', upstream, attended, preferred_el...]
    unnamed x5 -> x4, waiting for transfers between devices: 88.5 us -> 0.73 us
    psum x1 -> x0, waiting for transfers between devices: 34.1 us -> none  [per_device(): weight_grad = lax.psum(grad_piece, 'seq')]
    all_gather x0 -> x1, waiting for transfers between devices: none -> 21.8 us  [per_device(): weight_grad = jnp.sum(lax.all_gather(grad_piece, 'seq'), axis=0)]
    unnamed x30 -> x28, local copies, waits for them, and re-layouts: 19.9 us -> 14.6 us
  transfers between devices with their start and end apart: 4 -> 4, of which waited for: 4 -> 4; matrix products, arithmetic and copies ran while one was open for 16% -> 15% of each run, Pallas kernels for 0% -> 0%
where the time goes in v1:
time: 276 us; the launch traced here: 275 us
  waiting for transfers between devices  171 us (62%)
  local copies, waits for them, and re-layouts  24.7 us (9%)
  blocking collectives  23.7 us (9%)
  matrix products  21.4 us (8%)
  other arithmetic  20.1 us (7%)
  between operations  14 us (5%)
    reduce_scatter x1, waiting for transfers between devices, per_device(): lax.psum_scatter(jnp.einsum('io,id->od', upstream, attended, preferred_el...  94 us
    reduce_scatter x1, waiting for transfers between devices, per_device(): lax.psum_scatter(jnp.concatenate([key_part.reshape(row_count * lax.axis_s...  39.2 us
    all_gather x1, waiting for transfers between devices, per_device(): weight_grad = jnp.sum(lax.all_gather(grad_piece, 'seq'), axis=0)  21.8 us
    all_gather x1, waiting for transfers between devices, per_device(): full_weight = lax.all_gather(out_weight, 'dp', axis=0, tiled=True)  15.7 us
    unnamed x28, local copies, waits for them, and re-layouts  14.6 us
    all_gather x1, blocking collectives, per_device(): lax.all_gather(values, 'seq', axis=0, tiled=True)  12.8 us
    all_gather x1, blocking collectives, per_device(): lax.all_gather(keys, 'seq', axis=0, tiled=True)  11 us
  transfers between devices with their start and end apart: 4, of which 4 were waited for; matrix products, arithmetic and copies ran while one was open for 15% of the time, Pallas kernels for 0%

profile of v1, /device:TPU:0, one launch (start us, length us, event | category | flops | bytes accessed | tf_op | source)
XLA Modules:
  0.0 275.4 jit_solution(1486163967227236075)
XLA Ops:
  7.2 0.0 copy-start
  7.2 0.0 copy-start.7
  7.2 0.0 all-gather.4.cloned.1.call-start
  7.2 0.7 all-gather.4.cloned.1.call-update
  7.9 0.0 reduce-scatter.7.cloned.1.call-start
  8.0 1.0 slice_reduce_fusion.1
  9.0 0.1 reduce
  9.1 1.2 copy.46
  10.4 0.0 copy-start.3
  10.4 1.4 copy.47
  11.7 0.0 copy-done.7
  11.8 0.0 copy-start.10
  11.8 12.8 %all_gather.16 = bf16[256,1536]{1,0:T(8,128)(2,1)S(1)} all-gather(bf16[128,1536]{1,0:T(8,128)(2,1)S(1)} %copy-done.7), channel_id=1, replica_groups=mesh['dp'=16,'seq'=2] {'seq'}, dimensions={0}, use_global_device_ids=true | all-gather | bytes 1179648 | tf_op jit(solution)/shard_map/all_gather | solution.py:56
  24.5 1.2 copy.50
  25.7 0.0 copy-done.10
  25.7 0.1 constant_dynamic-slice_fusion
  25.8 0.7 fusion.18
  26.5 2.5 fusion.16
  29.0 0.6 fusion.19
  29.6 4.4 %compare_select_fusion.1 = s32[256,1]{0,1:T(1,128)S(1)} fusion(s32[]{:T(128)} %bitcast.7, s32[]{:T(128)} %bitcast.8, s32[]{:T(128)} %bitcast.9, s32[]{:T(128)} %bitcast.10, s32[]{:T(128)} %bitcast.11, s32[]{:T(128)} %bitcast.13, s32[]{:T(128)} %bitcast.12), kind=kLoop, calls=%fused_computation.30 | loop fusion | flops 5888 | bytes 1052 | tf_op jit(solution)/shard_map/gather | solution.py:49
  34.1 0.1 fusion.15
  34.2 0.6 broadcast_select_fusion
  34.8 0.1 fusion.14
  34.9 0.1 select_reduce_fusion.3
  35.0 0.1 select_reduce_fusion
  35.1 11.0 %all_gather.15 = bf16[256,1536]{0,1:T(8,128)(2,1)S(1)} all-gather(bf16[128,1536]{0,1:T(8,128)(2,1)S(1)} %copy.47), channel_id=1, replica_groups=mesh['dp'=16,'seq'=2] {'seq'}, dimensions={0}, use_global_device_ids=true | all-gather | bytes 1179648 | tf_op jit(solution)/shard_map/all_gather | solution.py:55
  46.1 2.8 %and_select_fusion.8 = (s32[128]{0:T(128)S(1)}, s32[128]{0:T(128)S(1)}, s32[128]{0:T(128)S(1)}) fusion(s32[128]{0:T(128)S(1)} %get-tuple-element.32, s32[128]{0:T(128)S(1)} %get-tuple-element.31, s32[128]{0:T(128)S(1)} %get-tuple-element.33, s32[]{:T(128)} %bitcast.3, s32[]{:T(128)} %bitcast.2, s32[]{:T(128)} %bitcast.1, s32[]{:T(128)} %bitcast), kind=kLoop, calls=%fused_computation.61 | loop fusion | flops 7168 | bytes 3088 | tf_op jit(solution)/shard_map/jit(floor_divide)/jit(_where)/select_n | solution.py:24
  48.8 0.3 and_select_fusion.7
  49.1 0.2 fusion.13
  49.3 0.0 copy-done.3
  49.3 0.5 fusion.20
  49.8 0.5 fusion
  50.3 0.0 copy-start.8
  50.3 15.7 %all-gather.4.cloned.1.call-done = bf16[1536,1536]{1,0:T(8,128)(2,1)} async-done(((bf16[96,1536]{1,0:T(8,128)(2,1)}), bf16[1536,1536]{1,0:T(8,128)(2,1)}) %all-gather.4.cloned.1.call-update) | async-done | bytes 4718608 | tf_op jit(solution)/shard_map/all_gather | solution.py:53
  66.0 0.0 copy-done
  66.0 3.1 %convolution_convert_fusion = bf16[128,1536]{1,0:T(8,128)(2,1)S(1)} fusion(bf16[128,1536]{1,0:T(8,128)(2,1)S(1)} %copy-done, bf16[1536,1536]{1,0:T(8,128)(2,1)} %all-gather.4.cloned.1.call-done), kind=kOutput, calls=%fused_computation.2 | convolution fusion | flops 604176384 | bytes 5505024 | tf_op jit(solution)/shard_map/dot_general | solution.py:78
  69.1 0.2 copy.51
  69.3 0.0 copy-start.2
  69.3 2.4 multiply_reduce_fusion
  71.7 0.7 copy-done.5
  72.5 5.0 %convolution_bitcast_fusion = f32[1536,1536]{0,1:T(8,128)} fusion(bf16[128,1536]{0,1:T(8,128)(2,1)S(1)} %bitcast.71, bf16[128,1536]{1,0:T(8,128)(2,1)S(1)} %copy-done), kind=kOutput, calls=%fused_computation | convolution fusion | flops 603979776 | bytes 10223616 | tf_op jit(solution)/shard_map/io,id->od/dot_general | solution.py:118
  77.5 9.6 %copy.62 = f32[1536,1536]{1,0:T(8,128)} copy(f32[1536,1536]{0,1:T(8,128)} %convolution_bitcast_fusion) | data formatting | bytes 18874368
  87.1 0.0 reduce-scatter.7.cloned.1.call-update
  87.2 0.0 reduce-scatter.5.cloned.1.call-start
  87.2 0.6 copy-done.9
  87.9 0.0 copy-done.2
  87.9 1.6 fusion.6
  89.5 3.1 %copy.55 = f32[256,1536]{1,0:T(8,128)} copy(f32[256,1536]{0,1:T(8,128)} %bitcast.62) | data formatting | bytes 3145728 | tf_op jit(solution)/shard_map/reshape | solution.py:107
  92.5 2.1 multiply_convert_fusion
  94.7 1.5 convolution_multiply_fusion
  96.2 3.4 %copy.54 = f32[256,1536]{1,0:T(8,128)} copy(f32[256,1536]{0,1:T(8,128)} %bitcast.63) | data formatting | bytes 3145728 | tf_op jit(solution)/shard_map/reshape | solution.py:106
  99.5 3.5 %pad_maximum_fusion = f32[256,3072]{1,0:T(8,128)} fusion(f32[256,1536]{1,0:T(8,128)S(1)} %copy-done.1, f32[256,1536]{1,0:T(8,128)} %copy.54), kind=kLoop, calls=%fused_computation.1 | loop fusion | flops 786432 | bytes 6291456 | tf_op jit(solution)/shard_map/concatenate | solution.py:104
  103.0 0.0 reduce-scatter.5.cloned.1.call-update
  103.0 0.0 all-gather.6.cloned.1.call-start
  103.1 94.0 %reduce-scatter.7.cloned.1.call-done = f32[96,1536]{1,0:T(8,128)} async-done(((f32[1536,1536]{1,0:T(8,128)}), f32[96,1536]{1,0:T(8,128)}) %reduce-scatter.7.cloned.1.call-update) | async-done | bytes 589840 | tf_op jit(solution)/shard_map/reduce_scatter | solution.py:117
  197.1 0.0 all-gather.6.cloned.1.call-update
  197.1 0.4 fusion.4
  197.5 0.9 copy.57
  198.4 4.7 %convolution_convert_fusion.1 = bf16[128,1536]{1,0:T(8,128)(2,1)} fusion(bf16[128,1536]{0,1:T(8,128)(2,1)S(1)} %bitcast.72, bf16[1536,1536]{1,0:T(8,128)(2,1)} %all-gather.4.cloned.1.call-done), kind=kOutput, calls=%fused_computation.3 | convolution fusion | flops 604176384 | bytes 5505024 | tf_op jit(solution)/shard_map/id,od->io/dot_general | solution.py:75
  203.2 39.2 %reduce-scatter.5.cloned.1.call-done = f32[128,3072]{1,0:T(8,128)} async-done(((f32[256,3072]{1,0:T(8,128)}), f32[128,3072]{1,0:T(8,128)}) %reduce-scatter.5.cloned.1.call-update) | async-done | bytes 1572880 | tf_op jit(solution)/shard_map/reduce_scatter | solution.py:103
  242.4 1.5 convert.4
  243.9 0.9 fusion.17
  244.9 21.8 %all-gather.6.cloned.1.call-done = f32[192,1536]{1,0:T(8,128)} async-done(((f32[96,1536]{1,0:T(8,128)}), f32[192,1536]{1,0:T(8,128)}) %all-gather.6.cloned.1.call-update) | async-done | bytes 1179664 | tf_op jit(solution)/shard_map/all_gather | solution.py:123
  266.6 2.2 reduce_sum.109
  (17 shorter events, 0.1 us)
Async XLA Ops:
  7.2 58.8 %copy-start = (bf16[128,1536]{1,0:T(8,128)(2,1)S(1)}, bf16[128,1536]{1,0:T(8,128)(2,1)}, u32[]{:S(2)}) copy-start(bf16[128,1536]{1,0:T(8,128)(2,1)} %param.10) | copy-start | bytes 1179652
  7.2 4.6 %copy-start.7 = (bf16[128,1536]{1,0:T(8,128)(2,1)S(1)}, bf16[128,1536]{1,0:T(8,128)(2,1)}, u32[]{:S(2)}) copy-start(bf16[128,1536]{1,0:T(8,128)(2,1)} %param.9) | copy-start | bytes 1179652
  7.2 58.8 %all-gather.4.cloned.1.call-start = ((), (), s32[]{:S(2)}) async-start(), calls=%async_computation.2 | async-start | bytes 5013504 | tf_op jit(solution)/shard_map/all_gather | solution.py:53
  7.9 189.2 %reduce-scatter.7.cloned.1.call-start = ((), (), s32[]{:S(2)}) async-start(), calls=%async_computation.5 | async-start | bytes 10027008 | tf_op jit(solution)/shard_map/reduce_scatter | solution.py:117
  10.4 38.9 %copy-start.3 = (bf16[128,1536]{0,1:T(8,128)(2,1)}, bf16[128,1536]{0,1:T(8,128)(2,1)S(1)}, u32[]{:S(2)}) copy-start(bf16[128,1536]{0,1:T(8,128)(2,1)S(1)} %copy.46) | copy-start | bytes 1179652
  11.8 14.0 %copy-start.10 = (s32[1,8]{1,0:T(1,128)S(1)}, s32[1,8]{1,0:T(1,128)}, u32[]{:S(2)}) copy-start(s32[1,8]{1,0:T(1,128)} %param.13) | copy-start | bytes 100
  50.3 19.0 %copy-start.8 = (f32[12,128]{1,0:T(8,128)}, f32[12,128]{1,0:T(8,128)S(1)}, u32[]{:S(2)}) copy-start(f32[12,128]{1,0:T(8,128)S(1)} %fusion) | copy-start | bytes 18436
  69.3 18.5 %copy-start.2 = (bf16[128,1536]{0,1:T(8,128)(2,1)}, bf16[128,1536]{0,1:T(8,128)(2,1)S(1)}, u32[]{:S(2)}) copy-start(bf16[128,1536]{0,1:T(8,128)(2,1)S(1)} %copy.51) | copy-start | bytes 1179652
  71.7 0.7 copy-start.5
  87.1 0.7 copy-start.9
  87.2 155.3 %reduce-scatter.5.cloned.1.call-start = ((), (), s32[]{:S(2)}) async-start(), calls=%async_computation.3 | async-start | bytes 4718592 | tf_op jit(solution)/shard_map/reduce_scatter | solution.py:103
  89.5 3.1 %copy-start.11 = (f32[128,12]{0,1:T(8,128)S(1)}, f32[128,12]{0,1:T(8,128)}, u32[]{:S(2)}) copy-start(f32[128,12]{0,1:T(8,128)} %get-tuple-element.57) | copy-start | bytes 18436
  92.5 2.1 copy-start.4
  96.2 3.4 %copy-start.1 = (f32[256,1536]{1,0:T(8,128)S(1)}, f32[256,1536]{1,0:T(8,128)}, u32[]{:S(2)}) copy-start(f32[256,1536]{1,0:T(8,128)} %copy.55) | copy-start | bytes 4718596
  103.0 163.6 %all-gather.6.cloned.1.call-start = ((), (), s32[]{:S(2)}) async-start(), calls=%async_computation.4 | async-start | bytes 1769472 | tf_op jit(solution)/shard_map/all_gather | solution.py:123
  197.1 1.3 copy-start.6
Sparse Core Ops, SparseCore 0:
  10.3 55.6 all-gather.3
  87.3 109.7 reduce-scatter.6
  199.3 43.0 reduce-scatter.4
  243.8 22.7 all-gather.5
